TPU v7x, 32 devices: a whole 2x2x4 slice. The times are simulated.
32 devices in a mesh: groups: 2 (over y), expo: 4 (over z), tile: 4 (over x, core).
Axes of the slice: x: 2, y: 2, z: 4, core: 2. Of those that a mesh axis runs over, the one named last changes fastest.
Arguments:
- template: bfloat16 [8, 64, 4096], P(('groups', 'expo'), 'tile'), parts along dimension 0
- science: bfloat16 [8, 1, 64, 4096], P(('groups', 'expo'), None, 'tile'), parts along dimension 0
- plan: int32 [8], P('groups'), parts along dimension 0, may hold values from 0 to 3, as said below
- orders: int32 [6, 2], replicated, may hold values from 0 to 2
- coadd_weight: float32 [8, 1], P(('groups', 'expo')), parts along dimension 0, may hold values from 0.3 to 3
- intersection: int32 [8, 1], P(('groups', 'expo')), parts along dimension 0, may hold values 0 or 1
Outputs:
- coadd: float32 [2, 64, 4096], P('groups', 'tile', 'expo'), parts along dimension 0
- coeffs: float32 [8, 1, 13], P(('groups', 'expo')), parts along dimension 0
There are 2 independent parts, one for each index of `groups`. A program takes and returns all parts, laid end to end along the dimension named above; an argument that names none is the same for every part. Nothing has to cross between parts.
Inputs may be any that keep to these rules, and one draw needn't show every extreme that they name: `plan`: a permutation of the group's patch indices.
All inputs are finite; a program needn't handle non-finite values. No bound on the sum of `intersection` on one device may be relied on, other than what follows from the above.
Results may differ from a plain program's by a relative error of at most 0.0061.
Values may be sent and summed in bfloat16 or wider, within the bound.
A program may use at most 64 MiB of HBM per device.

v0:
```python
import jax
import jax.numpy as jnp
from jax import lax
from jax.sharding import PartitionSpec as P

HALF = 15
NB = 6
NU = 13


SIGMAS = (0.8, 1.4, 2.2, 3.0, 4.0, 5.5)
RIDGE = 0.05


def broadcast(block, axis, holder):
    block = jnp.where(lax.axis_index(axis) == holder, block, jnp.zeros_like(block))
    return lax.psum(block, axis)


def extended(x, sides, width):
    for axis, dim in sides:
        size, length = (lax.axis_size(axis), x.shape[dim])
        up = [(i, (i + 1) % size) for i in range(size - 1)]
        down = [(j, i) for i, j in up]
        last = lax.slice_in_dim(x, length - width, length, axis=dim)
        first = lax.slice_in_dim(x, 0, width, axis=dim)
        before = lax.ppermute(last, axis, up)
        after = lax.ppermute(first, axis, down)
        x = jnp.concatenate([before, x, after], axis=dim)
    return x


def make_filters(orders):
    taps_pos = jnp.arange(2 * HALF + 1).astype(jnp.float32) - HALF
    row_list = []
    col_list = []
    for basis in range(NB):
        sigma = SIGMAS[basis]
        envelope = jnp.exp(-taps_pos * taps_pos / (2.0 * sigma * sigma))

        def power(order):
            return jnp.where(order == 0, 1.0, jnp.where(order == 1, taps_pos, taps_pos * taps_pos))

        row_filter = envelope * power(orders[basis, 0])
        col_filter = envelope * power(orders[basis, 1])
        row_list.append(row_filter / jnp.sqrt(jnp.sum(row_filter * row_filter)))
        col_list.append(col_filter / jnp.sqrt(jnp.sum(col_filter * col_filter)))
    return (jnp.stack(row_list).astype(jnp.bfloat16), jnp.stack(col_list).astype(jnp.bfloat16))


def band_matrix(filters, out_len, in_len):
    offset = jnp.arange(in_len)[None, :] - jnp.arange(out_len)[:, None]
    taps_idx = jnp.arange(2 * HALF + 1)
    picks = (offset[:, :, None] == taps_idx[None, None, :]).astype(jnp.float32)
    band = jnp.einsum("ijt,kt->kij", picks, filters.astype(jnp.float32))
    return band.astype(jnp.bfloat16)


def per_device(template, science, plan, orders, coadd_weight, intersection):
    row_filters, col_filters = make_filters(orders)
    rows = template.shape[1]
    width = template.shape[2]
    blocks_count = width // 128
    steps_count = science.shape[1]
    row_band = band_matrix(row_filters, rows, rows + 2 * HALF)
    col_band = jnp.transpose(band_matrix(col_filters, 128, 128 + 2 * HALF), (0, 2, 1))
    column_pos = 2.0 * (jnp.arange(width).astype(jnp.float32) + 0.5) / width - 1.0
    pieces = []
    fitted = []
    for step in range(steps_count):
        owner_index = plan[step]
        received = broadcast(template[0], "expo", owner_index)
        padded = extended(received, (("tile", 0),), HALF)
        rowconv = jnp.einsum(
            "kij,jw->kiw", row_band, padded, preferred_element_type=jnp.float32
        ).astype(jnp.bfloat16)
        blocks = rowconv.reshape(NB, rows, blocks_count, 128)
        empty_rim = jnp.zeros((NB, rows, 1, HALF), jnp.bfloat16)
        previous = jnp.concatenate([empty_rim, blocks[:, :, :-1, 128 - HALF :]], axis=2)
        following = jnp.concatenate([blocks[:, :, 1:, :HALF], empty_rim], axis=2)
        window = jnp.concatenate([previous, blocks, following], axis=3)
        conv = jnp.einsum("krbj,kjc->krbc", window, col_band, preferred_element_type=jnp.float32)
        conv = conv.reshape(NB, rows, width)
        fields = jnp.concatenate(
            [conv, conv * column_pos, jnp.ones((1, rows, width), jnp.float32)], axis=0
        )
        fields = fields.reshape(NU, rows * width)
        exposure_image = science[0, step].astype(jnp.float32).reshape(rows * width)
        normal_local = jnp.dot(fields, fields.T, precision=lax.Precision.HIGHEST)
        project_local = jnp.dot(fields, exposure_image, precision=lax.Precision.HIGHEST)
        normal_matrix, projections = lax.psum((normal_local, project_local), "tile")
        normal_matrix = normal_matrix + RIDGE * (jnp.trace(normal_matrix) / NU) * jnp.eye(
            NU, dtype=jnp.float32
        )
        factor = jnp.linalg.cholesky(normal_matrix)
        coeffs = jax.scipy.linalg.cho_solve((factor, True), projections)
        model = jnp.dot(coeffs, fields, precision=lax.Precision.HIGHEST)
        difference = exposure_image - model
        weight_now = coadd_weight[0, step] * intersection[0, step].astype(jnp.float32)
        pieces.append((weight_now * difference).reshape(rows, width))
        fitted.append(coeffs)
    weighted = jnp.stack(pieces)
    received_parts = lax.all_to_all(weighted[None], "expo", split_axis=3, concat_axis=0, tiled=True)
    coadd = jnp.sum(received_parts, axis=0)
    return (coadd, jnp.stack(fitted)[None])


def solution(mesh):
    return jax.shard_map(
        per_device,
        mesh=mesh,
        in_specs=(
            P(("groups", "expo"), "tile", None),
            P(("groups", "expo"), None, "tile", None),
            P("groups"),
            P(),
            P(("groups", "expo"), None),
            P(("groups", "expo"), None),
        ),
        out_specs=(P("groups", "tile", "expo"), P(("groups", "expo"), None, None)),
        check_vma=False,
    )
```

profile of v0, /device:TPU:0, one launch (start us, length us, event | category | flops | bytes accessed | tf_op | source)
XLA Modules:
  0.0 144.9 jit_solution(105199897231821041)
XLA Ops:
  7.2 0.0 all-reduce.5.cloned.1.call-start
  7.9 0.7 select_bitcast_fusion
  8.5 0.0 all-reduce.5.cloned.1.call-update
  8.6 1.8 %fusion.124 = (s32[1,1]{0,1:T(1,128)}, s32[1,1]{0,1:T(1,128)}, s32[1,1]{0,1:T(1,128)}, s32[1,1]{0,1:T(1,128)}, s32[1,1]{0,1:T(1,128)}, /*index=5*/s32[1,1]{0,1:T...) fusion(s32[6,2]{0,1:T(2,128)} %param.9), kind=kLoop, calls=%fused_computation.211 | loop fusion | bytes 96 | tf_op jit(solution)/shard_map/slice | solution.py:45
  25.6 0.6 fusion.93
  26.9 0.6 fusion.113
  28.2 0.6 fusion.111
  29.5 0.6 fusion.109
  30.8 0.6 fusion.107
  32.1 0.6 fusion.105
  33.4 0.6 fusion.103
  34.7 0.6 fusion.101
  36.1 0.6 fusion.99
  37.4 0.6 fusion.97
  38.7 0.6 fusion.95
  40.0 0.6 fusion.91
  41.5 0.2 convolution_convert_fusion.1
  42.9 1.8 %copy.41 = bf16[1,1,16,4096]{3,1,2,0:T(2,128)(2,1)} copy(bf16[1,1,16,4096]{3,2,1,0:T(8,128)(2,1)} %param.7) | data formatting | bytes 262144
  44.8 0.9 copy.38
  45.7 0.1 copy.40
  45.8 0.6 pad.7.clone
  46.4 1.3 all-reduce.5.cloned.1.call-done
  47.7 1.0 fusion.123
  48.7 1.3 collective-permute-start
  50.0 1.3 collective-permute-start.1
  51.3 0.5 fusion.21
  51.8 0.0 collective-permute-done
  51.8 3.4 %collective-permute-done.1 = bf16[15,4096]{1,0:T(8,128)(2,1)S(1)} collective-permute-done((bf16[15,4096]{1,0:T(8,128)(2,1)S(1)}, bf16[15,4096]{1,0:T(8,128)(2,1)S(1)}, u32[]{:S(2)}, u32[]{:S(2)}) %collective-permute-start.1) | collective-permute-done | bytes 122912 | tf_op jit(solution)/shard_map/ppermute | solution.py:28
  55.2 1.3 convolution_convert_fusion
  56.5 0.2 copy.37
  56.6 0.6 fusion.122
  57.2 1.5 %fusion.10 = f32[6,16,32,128]{3,2,1,0:T(8,128)S(1)} fusion(bf16[6,16,31,15]{3,2,1,0:T(8,128)(2,1)S(1)} %get-tuple-element.9, bf16[6,16,31,15]{3,2,1,0:T(8,128)(2,1)S(1)} %get-tuple-element.8, bf16[6,16,32,128]{3,2,1,0:T(8,128)(2,1)S(1)} %bitcast.105, bf16[6,128,158,1]{1,0,2,3:T(8,128)(2,1)S(1)} %fusion.21), kind=kOutput, calls=%fused_computation.17 | convolution fusion | flops 129110016 | bytes 2780544 | tf_op jit(solution)/shard_map/krbj,kjc->krbc/dot_general | solution.py:82
  58.7 0.3 reshape.337
  59.0 0.0 copy-start.4
  59.0 0.1 broadcast_multiply_fusion.1
  59.2 0.5 copy-done.4
  59.7 0.4 maximum_maximum_fusion.1
  60.1 6.5 %fusion.22 = f32[13,13]{1,0:T(8,128)S(1)} fusion(f32[13,16,4096]{2,1,0:T(8,128)S(1)} %maximum_maximum_fusion.1), kind=kOutput, calls=%fused_computation.28 | convolution fusion | flops 132907008 | bytes 3408548 | tf_op jit(solution)/shard_map/dot_general | solution.py:89
  66.6 1.0 copy.53
  67.6 0.0 copy-start
  67.6 1.0 broadcast_multiply_fusion
  68.6 0.3 copy-done
  68.9 1.0 copy-done.1
  69.9 3.3 %fusion.25 = f32[13]{0:T(128)S(1)} fusion(bf16[65536,1]{0,1:T(2,128)(2,1)S(1)} %bitcast.112, f32[6,65536]{1,0:T(8,128)S(1)} %broadcast_multiply_fusion, f32[6,65536]{1,0:T(8,128)S(1)} %bitcast.100, f32[13]{0:T(128)S(1)} %copy-done.4), kind=kOutput, calls=%fused_computation.30 | convolution fusion | flops 11927552 | bytes 3276904 | tf_op jit(solution)/shard_map/dot_general | solution.py:90
  73.2 9.7 %all-reduce.2 = (f32[13,13]{1,0:T(8,128)S(1)}, f32[13]{0:T(128)S(1)}) all-reduce(f32[13,13]{1,0:T(8,128)S(1)} %fusion.22, f32[13]{0:T(128)S(1)} %fusion.25), channel_id=1, replica_groups=mesh['groups'=2,'expo'=4,'tile'=4] {'tile'}, use_global_device_ids=true, to_apply=%region_13.14 | all-reduce | flops 182 | bytes 1456 | tf_op jit(solution)/shard_map/psum | solution.py:91
  82.9 0.6 select_reduce_fusion.1
  84.2 0.1 copy.31
  84.3 1.2 cholesky.17
  85.5 0.6 compare_reduce_fusion
  86.1 0.6 fusion.34
  86.8 1.0 custom-call.10
  87.8 0.1 convolution_bitcast_fusion
  87.9 0.1 fusion.35
  88.1 5.0 %fusion.2 = f32[1,65536]{1,0:T(1,128)S(1)} fusion(f32[6,65536]{1,0:T(8,128)} %copy-done.1, f32[6,65536]{1,0:T(8,128)} %bitcast.101, f32[13]{0:T(128)S(1)} %copy-done.5, f32[1,13]{1,0:T(1,128)S(1)} %fusion.35), kind=kOutput, calls=%fused_computation.5 | convolution fusion | flops 11927552 | bytes 3407976 | tf_op jit(solution)/shard_map/dot_general | solution.py:97
  93.2 0.1 broadcast_in_dim_stack_reshape.3
  93.2 2.5 %copy.32 = f32[1,1,16,4096]{2,1,0,3:T(1,128)S(1)} copy(f32[1,1,16,4096]{3,2,1,0:T(8,128)S(1)} %broadcast_in_dim_stack_reshape.3) | data formatting | bytes 524288 | tf_op jit(solution)/shard_map/broadcast_in_dim;stack;reshape | solution.py:103
  95.7 0.5 broadcast.809
  96.2 19.4 %reduce.10 = f32[4096,16]{1,0:T(8,128)} reduce(f32[4096,1,1,16]{3,2,1,0:T(1,128)S(1)} %bitcast.102, f32[]{:T(128)} %broadcast.809), dimensions={1,2}, to_apply=%bitcast.92.reduce_sub_computation | reduce | bytes 524292
  115.6 2.3 %reshape.354 = f32[4,1,16384]{2,1,0:T(1,128)S(1)} reshape(f32[4096,16]{1,0:T(8,128)} %reduce.10) | data formatting | bytes 524288
  117.9 14.1 %all_to_all.12 = f32[4,1,16384]{2,1,0:T(1,128)S(1)} all-to-all(f32[4,1,16384]{2,1,0:T(1,128)S(1)} %reshape.354), channel_id=1, replica_groups=mesh['groups'=2,'expo'=4,'tile'=4] {'expo'}, dimensions={0} | all-to-all | bytes 524288 | tf_op jit(solution)/shard_map/all_to_all | solution.py:103
  131.9 1.4 reduce.11
  133.3 3.7 %reshape.355 = f32[4096,1,1,16]{3,2,1,0:T(1,128)S(1)} reshape(f32[4,16384]{1,0:T(4,128)S(1)} %reduce.11) | data formatting | bytes 524288
  137.0 0.2 reduce_sum.142
  137.2 0.8 copy.33
  (23 shorter events, 0.3 us)
Async XLA Ops:
  7.2 40.5 %all-reduce.5.cloned.1.call-start = ((), (), s32[]{:S(2)}) async-start(), calls=%async_computation.1 | async-start | bytes 262144 | tf_op jit(solution)/shard_map/psum | solution.py:17
  48.7 3.1 %collective-permute-start = (bf16[15,4096]{1,0:T(8,128)(2,1)S(1)}, bf16[15,4096]{1,0:T(8,128)(2,1)S(1)}, u32[]{:S(2)}, u32[]{:S(2)}) collective-permute-start(bf16[15,4096]{1,0:T(8,128)(2,1)S(1)} %get-tuple-element.10), channel_id=1, source_target_pairs={{0,1},{1,2},{2,3},{4,5},{5,6},{6,7},{8,9},{9,10},{10,11},{12,13},{... | collective-permute-start | bytes 368648 | tf_op jit(solution)/shard_map/ppermute | solution.py:27
  50.0 5.2 %collective-permute-start.1 = (bf16[15,4096]{1,0:T(8,128)(2,1)S(1)}, bf16[15,4096]{1,0:T(8,128)(2,1)S(1)}, u32[]{:S(2)}, u32[]{:S(2)}) collective-permute-start(bf16[15,4096]{1,0:T(8,128)(2,1)S(1)} %get-tuple-element.11), channel_id=1, source_target_pairs={{1,0},{2,1},{3,2},{5,4},{6,5},{7,6},{9,8},{10,9},{11,10},{13,12},{... | collective-permute-start | bytes 368648 | tf_op jit(solution)/shard_map/ppermute | solution.py:28
  59.0 0.7 copy-start.4
  67.6 1.3 copy-start
  67.6 2.3 %copy-start.2 = (bf16[1,1,16,4096]{3,1,2,0:T(2,128)(2,1)S(1)}, bf16[1,1,16,4096]{3,1,2,0:T(2,128)(2,1)}, u32[]{:S(2)}) copy-start(bf16[1,1,16,4096]{3,1,2,0:T(2,128)(2,1)} %copy.41) | copy-start | bytes 393220
  68.6 1.4 copy-start.1
  69.9 18.1 %copy-start.5 = (f32[13]{0:T(128)S(1)}, f32[13]{0:T(128)}, u32[]{:S(2)}) copy-start(f32[13]{0:T(128)} %pad.7.clone) | copy-start | bytes 160
  88.1 5.0 %copy-start.3 = (f32[1,13]{1,0:T(1,128)}, f32[1,13]{1,0:T(1,128)S(1)}, u32[]{:S(2)}) copy-start(f32[1,13]{1,0:T(1,128)S(1)} %fusion.35) | copy-start | bytes 160
Sparse Core Ops, SparseCore 0:
  10.3 37.3 all-reduce.4
where the time goes:
time: 145 us
  between operations  40.4 us (28%)
  other arithmetic  34.7 us (24%)
  blocking collectives  23.7 us (16%)
  local copies, waits for them, and re-layouts  20.1 us (14%)
  matrix products  18.6 us (13%)
  waiting for transfers between devices  4.66 us (3%)
  starting transfers between devices  2.63 us (2%)
    unnamed x1, other arithmetic  19.4 us
    all_to_all x1, blocking collectives, per_device(): lax.all_to_all(weighted[None], 'expo', split_axis=3, concat_axis=0, tiled...  14.1 us
    unnamed x22, local copies, waits for them, and re-layouts  13.1 us
    psum x1, blocking collectives, per_device(): normal_matrix, projections = lax.psum((normal_local, project_local), 'tile')  9.66 us
    dot_general x1, matrix products, per_device(): normal_local = jnp.dot(fields, fields.T, precision=lax.Precision.HIGHEST)  6.53 us
    dot_general x1, matrix products, per_device(): model = jnp.dot(coeffs, fields, precision=lax.Precision.HIGHEST)  5.02 us
    reduce_sum x6, other arithmetic, make_filters(): col_list.append(col_filter / jnp.sqrt(jnp.sum(col_filter * col_filter)))  3.69 us
    reduce_sum x6, other arithmetic, make_filters(): row_list.append(row_filter / jnp.sqrt(jnp.sum(row_filter * row_filter)))  3.69 us
  transfers between devices with their start and end apart: 3, of which 2 were waited for; matrix products, arithmetic and copies ran while one was open for 9% of the time, Pallas kernels for 0%

commit v1 on v0

--- a/solution.py
+++ b/solution.py
@@ -1,6 +1,10 @@
+import functools
+
 import jax
 import jax.numpy as jnp
 from jax import lax
+from jax.experimental import pallas as pl
+from jax.experimental.pallas import tpu as pltpu
 from jax.sharding import PartitionSpec as P
 
 HALF = 15
@@ -105,9 +109,426 @@
     return (coadd, jnp.stack(fitted)[None])
 
 
+LANES = 128
+WIDE = 256
+PAIRS = [(u, v) for u in range(NB) for v in range(u + 1)]
+MESH = pl.DeviceIdType.MESH
+
+
+def taps(position, sigma, order):
+    power = jnp.where(order == 0, 1.0, jnp.where(order == 1, position, position * position))
+    value = jnp.exp(-position * position / (2.0 * sigma * sigma)) * power
+    return jnp.where(jnp.abs(position) <= HALF, value, 0.0)
+
+
+def fused(
+    dims,
+    template_ref,
+    science_ref,
+    plan_ref,
+    orders_ref,
+    weight_ref,
+    inter_ref,
+    coadd_ref,
+    coeffs_ref,
+    tbuf,
+    sbuf,
+    rbuf,
+    row_band,
+    col_band,
+    conv_ref,
+    stat_ref,
+    local_sem,
+    tsend,
+    trecv,
+    ssend,
+    srecv,
+    fsend,
+    frecv,
+    rsend,
+    rrecv,
+):
+    expos, tiles, rows, width, cols = dims
+    per = cols // LANES
+    span = cols + 2 * LANES
+    blocks = cols // WIDE
+    chunks = [(b, h) for b in range(blocks) for h in range(WIDE // LANES)]
+    me = lax.axis_index("expo")
+    tile = lax.axis_index("tile")
+
+    def others():
+        for de in range(expos):
+            for dt in range(tiles):
+                if de or dt:
+                    yield de * tiles + dt, (me + de) % expos, (tile + dt) % tiles
+
+    barrier = pltpu.get_barrier_semaphore()
+    for _, e, t in others():
+        pl.semaphore_signal(
+            barrier, inc=1, device_id={"expo": e, "tile": t}, device_id_type=MESH
+        )
+
+    def source_start(e):
+        return e * per - 1 + (expos - 1 - e) // (expos - 1) - e // (expos - 1)
+
+    def source_columns(e):
+        return pl.ds(pl.multiple_of(source_start(e) * LANES, LANES), span)
+
+    def window_columns(e):
+        return pl.ds(pl.multiple_of((source_start(e) - e * per + 2) * LANES, LANES), span)
+
+    def own_columns(e):
+        return pl.ds(pl.multiple_of(e * cols, LANES), cols)
+
+    mine = pltpu.make_async_copy(
+        template_ref.at[0, :, source_columns(me)],
+        tbuf.at[me, 1, :, window_columns(me)],
+        local_sem.at[0],
+    )
+    mine.start()
+    mine_science = pltpu.make_async_copy(
+        science_ref.at[0, 0, :, own_columns(me)], sbuf.at[me], local_sem.at[1]
+    )
+    mine_science.start()
+    pl.semaphore_wait(barrier, expos * tiles - 1)
+
+    def template_copy(d, target, holder):
+        return pltpu.make_async_remote_copy(
+            src_ref=template_ref.at[0, :, source_columns(target)],
+            dst_ref=tbuf.at[holder, 1, :, window_columns(target)],
+            send_sem=tsend.at[d],
+            recv_sem=trecv.at[d],
+            device_id={"expo": target},
+            device_id_type=MESH,
+        )
+
+    def science_copy(d, target, holder):
+        return pltpu.make_async_remote_copy(
+            src_ref=science_ref.at[0, 0, :, own_columns(target)],
+            dst_ref=sbuf.at[holder],
+            send_sem=ssend.at[d],
+            recv_sem=srecv.at[d],
+            device_id={"expo": target},
+            device_id_type=MESH,
+        )
+
+    def forward_copy(d, holder, side):
+        target = tile + 1 if side == 0 else tile - 1
+        return pltpu.make_async_remote_copy(
+            src_ref=tbuf.at[holder, 1, :, window_columns(me)],
+            dst_ref=tbuf.at[holder, 2 * side, :, window_columns(me)],
+            send_sem=fsend.at[side, d],
+            recv_sem=frecv.at[side, d],
+            device_id={"tile": target},
+            device_id_type=MESH,
+        )
+
+    def forward(d, holder):
+        @pl.when(tile < tiles - 1)
+        def _():
+            forward_copy(d, holder, 0).start()
+
+        @pl.when(tile > 0)
+        def _():
+            forward_copy(d, holder, 1).start()
+
+    for d in range(1, expos):
+        template_copy(d, (me + d) % expos, me).start()
+    mine.wait()
+    forward(0, me)
+    for d in range(1, expos):
+        science_copy(d, (me + d) % expos, me).start()
+
+    position = lax.broadcasted_iota(jnp.int32, (1, LANES), 1).astype(jnp.float32) - HALF
+    for k in range(NB):
+        sigma = SIGMAS[k]
+        for side, length in ((0, rows), (1, LANES)):
+            order = jnp.full((1, LANES), orders_ref[k, side], jnp.int32)
+            line = taps(position, sigma, order)
+            root = jnp.sqrt(jnp.sum(line * line, axis=1, keepdims=True))
+            scale = 1.0 / root
+            if side == 0:
+                shape = (rows, 3 * rows)
+                offset = (
+                    lax.broadcasted_iota(jnp.int32, shape, 1)
+                    - lax.broadcasted_iota(jnp.int32, shape, 0)
+                    - rows
+                ).astype(jnp.float32)
+                band = taps(offset, sigma, jnp.full(shape, orders_ref[k, side], jnp.int32))
+                row_band[k * rows : (k + 1) * rows, :] = (band * scale).astype(jnp.bfloat16)
+            else:
+                shape = (LANES, LANES)
+                delta = lax.broadcasted_iota(jnp.int32, shape, 0) - lax.broadcasted_iota(
+                    jnp.int32, shape, 1
+                )
+                column_order = jnp.full(shape, orders_ref[k, side], jnp.int32)
+                zero = jnp.zeros(shape, jnp.bfloat16)
+                parts = {}
+                for kind in range(3):
+                    offset = (delta + (kind - 1) * LANES).astype(jnp.float32)
+                    band = taps(offset, sigma, column_order)
+                    parts[kind] = (band * scale).astype(jnp.bfloat16)
+                for jb in range(WIDE // LANES + 2):
+                    for cb in range(WIDE // LANES):
+                        col_band[
+                            k,
+                            jb * LANES : (jb + 1) * LANES,
+                            cb * LANES : (cb + 1) * LANES,
+                        ] = parts.get(jb - cb, zero)
+
+    for d in range(1, expos):
+        holder = (me + expos - d) % expos
+        template_copy(d, me, holder).wait_recv()
+        forward(d, holder)
+
+    @pl.when(tile > 0)
+    def _():
+        for d in range(expos):
+            forward_copy(d, (me + expos - d) % expos, 0).wait_recv()
+
+    @pl.when(tile < tiles - 1)
+    def _():
+        for d in range(expos):
+            forward_copy(d, (me + expos - d) % expos, 1).wait_recv()
+
+    @pl.when(tile < tiles - 1)
+    def _():
+        for d in range(expos):
+            forward_copy(d, (me + expos - d) % expos, 0).wait_send()
+
+    @pl.when(tile > 0)
+    def _():
+        for d in range(expos):
+            forward_copy(d, (me + expos - d) % expos, 1).wait_send()
+
+    owner = plan_ref[0]
+    shape = (rows, span)
+    column = lax.broadcasted_iota(jnp.int32, shape, 1) + (me * cols - LANES)
+    inside = (column >= 0) & (column < width)
+    pieces = []
+    for part in range(3):
+        block = tbuf[owner, part, :, LANES : LANES + span].astype(jnp.float32)
+        keep = inside
+        if part == 0:
+            keep = keep & (jnp.full(shape, tile, jnp.int32) > 0)
+        if part == 2:
+            keep = keep & (jnp.full(shape, tile, jnp.int32) < tiles - 1)
+        pieces.append(jnp.where(keep, block, 0.0).astype(jnp.bfloat16))
+    rows_window = jnp.concatenate(pieces, axis=0)
+    rowconv = jnp.dot(
+        row_band[...], rows_window, preferred_element_type=jnp.float32
+    ).astype(jnp.bfloat16)
+    for k in range(NB):
+        mine_rows = rowconv[k * rows : (k + 1) * rows]
+        windows = jnp.concatenate(
+            [mine_rows[:, b * WIDE : (b + 1) * WIDE + 2 * LANES] for b in range(blocks)], axis=0
+        )
+        conv_ref[k] = jnp.dot(windows, col_band[k], preferred_element_type=jnp.float32)
+
+    def conv_at(k, b, h):
+        return conv_ref[k, b * rows : (b + 1) * rows, h * LANES : (h + 1) * LANES]
+
+    def science_at(e, b, h):
+        start = b * WIDE + h * LANES
+        return sbuf[e, :, start : start + LANES].astype(jnp.float32)
+
+    def fold(x):
+        return x.reshape(rows // 8, 8, LANES).sum(axis=0)
+
+    lane = lax.broadcasted_iota(jnp.int32, (1, LANES), 1)
+    columns = {}
+    for b, h in chunks:
+        place = (me * cols + b * WIDE + h * LANES + lane).astype(jnp.float32)
+        columns[b, h] = 2.0 * (place + 0.5) / width - 1.0
+
+    def put(index, value):
+        stat_ref[index : index + 1, :] = jnp.sum(value, axis=0, keepdims=True)
+
+    count = 3 * len(PAIRS) + 2 * NB
+    for index, (u, v) in enumerate(PAIRS):
+        sums = [0.0, 0.0, 0.0]
+        for b, h in chunks:
+            product = fold(conv_at(u, b, h) * conv_at(v, b, h))
+            once = product * columns[b, h]
+            sums = [sums[0] + product, sums[1] + once, sums[2] + once * columns[b, h]]
+        for moment in range(3):
+            put(3 * index + moment, sums[moment])
+    for u in range(NB):
+        sums = [0.0, 0.0]
+        for b, h in chunks:
+            product = fold(conv_at(u, b, h))
+            sums = [sums[0] + product, sums[1] + product * columns[b, h]]
+        for moment in range(2):
+            put(3 * len(PAIRS) + NB * moment + u, sums[moment])
+
+    mine_science.wait()
+    for d in range(1, expos):
+        science_copy(d, me, (me + expos - d) % expos).wait_recv()
+    for e in range(expos):
+        for u in range(NB):
+            sums = [0.0, 0.0]
+            for b, h in chunks:
+                product = fold(conv_at(u, b, h) * science_at(e, b, h))
+                sums = [sums[0] + product, sums[1] + product * columns[b, h]]
+            for moment in range(2):
+                put(count + (NB * moment + u) * expos + e, sums[moment])
+        total = 0.0
+        for b, h in chunks:
+            total = total + fold(science_at(e, b, h))
+        put(count + 2 * NB * expos + e, total)
+    used = count + NU * expos
+    if used < LANES:
+        stat_ref[used:LANES, :] = jnp.zeros((LANES - used, LANES), jnp.float32)
+
+    reduced = jnp.sum(jnp.transpose(stat_ref[...]), axis=0, keepdims=True)
+    weight = weight_ref[0, 0] * inter_ref[0, 0].astype(jnp.float32)
+    rbuf[me, tile, :, :LANES] = reduced
+    rbuf[me, tile, :, LANES:] = jnp.full((1, LANES), weight, jnp.float32)
+
+    def stat_copy(index, e, t, to_e, to_t):
+        return pltpu.make_async_remote_copy(
+            src_ref=rbuf.at[e, t],
+            dst_ref=rbuf.at[e, t],
+            send_sem=rsend.at[index],
+            recv_sem=rrecv.at[index],
+            device_id={"expo": to_e, "tile": to_t},
+            device_id_type=MESH,
+        )
+
+    for index, e, t in others():
+        stat_copy(index, me, tile, e, t).start()
+    for d in range(1, expos):
+        template_copy(d, (me + d) % expos, me).wait_send()
+        science_copy(d, (me + d) % expos, me).wait_send()
+    for de in range(expos):
+        for dt in range(tiles):
+            if de or dt:
+                e = (me + expos - de) % expos
+                t = (tile + tiles - dt) % tiles
+                stat_copy(de * tiles + dt, e, t, e, t).wait_recv()
+
+    total = rbuf[0, 0, :, :LANES]
+    for e in range(expos):
+        for t in range(tiles):
+            if e or t:
+                total = total + rbuf[e, t, :, :LANES]
+    stat_ref[...] = jnp.transpose(jnp.broadcast_to(total, (LANES, LANES)))
+
+    def value(index):
+        return jnp.broadcast_to(stat_ref[index : index + 1, :], (expos, LANES))
+
+    matrix = [[None] * NU for _ in range(NU)]
+    for index, (u, v) in enumerate(PAIRS):
+        plain, once, twice = (value(3 * index + moment) for moment in range(3))
+        matrix[u][v] = plain
+        matrix[NB + u][v] = once
+        matrix[NB + v][u] = once
+        matrix[NB + u][NB + v] = twice
+    for u in range(2 * NB):
+        matrix[2 * NB][u] = value(3 * len(PAIRS) + u)
+    pixels = float(rows * tiles * width)
+    matrix[2 * NB][2 * NB] = jnp.full((expos, LANES), pixels, jnp.float32)
+    trace = matrix[0][0]
+    for u in range(1, NU):
+        trace = trace + matrix[u][u]
+    ridge = RIDGE * (trace / NU)
+    for u in range(NU):
+        matrix[u][u] = matrix[u][u] + ridge
+    right = [stat_ref[count + u * expos : count + (u + 1) * expos, :] for u in range(NU)]
+    inverse = [None] * NU
+    for j in range(NU):
+        inverse[j] = 1.0 / matrix[j][j]
+        for i in range(j + 1, NU):
+            ratio = matrix[i][j] * inverse[j]
+            for m in range(j + 1, i + 1):
+                matrix[i][m] = matrix[i][m] - ratio * matrix[m][j]
+            right[i] = right[i] - ratio * right[j]
+    fitted = [None] * NU
+    for j in reversed(range(NU)):
+        left = right[j]
+        for i in range(j + 1, NU):
+            left = left - matrix[i][j] * fitted[i]
+        fitted[j] = left * inverse[j]
+
+    spread = lax.broadcasted_iota(jnp.int32, (expos, LANES), 1)
+    table = jnp.zeros((expos, LANES), jnp.float32)
+    for u in range(NU):
+        table = jnp.where(spread == u, fitted[u], table)
+    exposure = lax.broadcasted_iota(jnp.int32, (expos, LANES), 0)
+    line = jnp.sum(jnp.where(exposure == me, table, 0.0), axis=0, keepdims=True)
+    coeffs_ref[0] = line[:, :NU]
+
+    weights = [rbuf[e, tile, :, LANES:] for e in range(expos)]
+    stacked = jnp.concatenate(weights, axis=0)
+    joint = [jnp.sum(stacked * fitted[u], axis=0, keepdims=True) for u in range(NU)]
+    for b, h in chunks:
+        result = science_at(0, b, h) * weights[0]
+        for e in range(1, expos):
+            result = result + science_at(e, b, h) * weights[e]
+        result = result - joint[2 * NB]
+        for k in range(NB):
+            factor = joint[k] + columns[b, h] * joint[NB + k]
+            result = result - conv_at(k, b, h) * factor
+        start = b * WIDE + h * LANES
+        coadd_ref[0, :, start : start + LANES] = result
+    for index, e, t in others():
+        stat_copy(index, me, tile, e, t).wait_send()
+
+
+def window(sizes, template, science, plan, orders, coadd_weight, intersection):
+    expos, tiles = (sizes["expo"], sizes["tile"])
+    rows, width = template.shape[1:]
+    cols = width // expos
+    fits = (
+        science.shape[1] == 1
+        and template.shape[0] == 1
+        and expos > 1
+        and width % expos == 0
+        and cols % WIDE == 0
+        and rows % 16 == 0
+        and 3 * len(PAIRS) + 2 * NB + NU * expos <= LANES
+    )
+    if not fits:
+        return per_device(template, science, plan, orders, coadd_weight, intersection)
+    span = cols + 4 * LANES
+    dims = (expos, tiles, rows, width, cols)
+    dma = pltpu.SemaphoreType.DMA
+    anywhere = pl.BlockSpec(memory_space=pl.ANY)
+    scalar = pl.BlockSpec(memory_space=pltpu.SMEM)
+    vector = pl.BlockSpec(memory_space=pltpu.VMEM)
+    return pl.pallas_call(
+        functools.partial(fused, dims),
+        out_shape=(
+            jax.ShapeDtypeStruct((1, rows, cols), jnp.float32),
+            jax.ShapeDtypeStruct((1, 1, NU), jnp.float32),
+        ),
+        in_specs=[anywhere, anywhere, scalar, scalar, scalar, scalar],
+        out_specs=(vector, vector),
+        scratch_shapes=[
+            pltpu.VMEM((expos, 3, rows, span), jnp.bfloat16),
+            pltpu.VMEM((expos, rows, cols), jnp.bfloat16),
+            pltpu.VMEM((expos, tiles, 1, 2 * LANES), jnp.float32),
+            pltpu.VMEM((NB * rows, 3 * rows), jnp.bfloat16),
+            pltpu.VMEM((NB, WIDE + 2 * LANES, WIDE), jnp.bfloat16),
+            pltpu.VMEM((NB, rows * (cols // WIDE), WIDE), jnp.float32),
+            pltpu.VMEM((LANES, LANES), jnp.float32),
+            dma((2,)),
+            dma((expos,)),
+            dma((expos,)),
+            dma((expos,)),
+            dma((expos,)),
+            dma((2, expos)),
+            dma((2, expos)),
+            dma((expos * tiles,)),
+            dma((expos * tiles,)),
+        ],
+        compiler_params=pltpu.CompilerParams(collective_id=0, has_side_effects=True),
+    )(template, science, plan, orders, coadd_weight, intersection)
+
+
 def solution(mesh):
     return jax.shard_map(
-        per_device,
+        functools.partial(window, dict(mesh.shape)),
         mesh=mesh,
         in_specs=(
             P(("groups", "expo"), "tile", None),

time: 145 us -> 27.1 us (0.19)
  between operations: 40.4 us -> 1.96 us
  other arithmetic: 34.7 us -> 0 us
  blocking collectives: 23.7 us -> 0 us
  Pallas kernels: 0 us -> 22.2 us
  matrix products: 18.6 us -> 0 us
  local copies, waits for them, and re-layouts: 20.1 us -> 2.68 us
  waiting for transfers between devices: 4.66 us -> 0 us
  starting transfers between devices: 2.63 us -> 0 us
    pallas_call x0 -> x1, Pallas kernels: none -> 22.2 us  [window(): pl.pallas_call(functools.partial(fused, dims), out_shape=(jax.ShapeDtypeS...]
    unnamed x1 -> x0, other arithmetic: 19.4 us -> none
    dot_general x7 -> x0, matrix products: 18.3 us -> none  [the longest x1 6.53 us: per_device(): normal_local = jnp.dot(fields, fields.T, precision=lax.Precision.HIGHEST)]
    all_to_all x1 -> x0, blocking collectives: 14.1 us -> none  [per_device(): lax.all_to_all(weighted[None], 'expo', split_axis=3, concat_axis=0, tiled...]
    unnamed x22 -> x7, local copies, waits for them, and re-layouts: 13.1 us -> 2.68 us
    psum x1 -> x0, blocking collectives: 9.66 us -> none  [per_device(): normal_matrix, projections = lax.psum((normal_local, project_local), 'tile')]
    reduce_sum x14 -> x0, other arithmetic: 8.16 us -> none  [the longest x6 3.69 us: make_filters(): col_list.append(col_filter / jnp.sqrt(jnp.sum(col_filter * col_filter)))]
    another operation x11 -> x0, other arithmetic: 3.6 us -> none  [the longest x3 1.85 us: per_device(): factor = jnp.linalg.cholesky(normal_matrix)]
  transfers between devices with their start and end apart: 3 -> 0, of which waited for: 2 -> 0; matrix products, arithmetic and copies ran while one was open for 9% -> 0% of each run, Pallas kernels for 0% -> 0%
where the time goes in v1:
time: 27.1 us; the launch traced here: 26.8 us
  Pallas kernels  22.2 us (82%)
  local copies, waits for them, and re-layouts  2.68 us (10%)
  between operations  1.96 us (7%)
    pallas_call x1, Pallas kernels, window(): pl.pallas_call(functools.partial(fused, dims), out_shape=(jax.ShapeDtypeS...  22.2 us
    unnamed x7, local copies, waits for them, and re-layouts  2.68 us

profile of v1, /device:TPU:0, one launch (start us, length us, event | category | flops | bytes accessed | tf_op | source)
XLA Modules:
  0.0 26.8 jit_solution(10071451458049076577)
XLA Ops:
  1.3 0.0 copy-start
  1.9 0.0 copy-done
  2.0 0.7 %copy.8.orders_ref = s32[6,2]{1,0:T(8,128)} copy(s32[6,2]{0,1:T(2,128)S(1)} %copy-done) | data formatting | bytes 96 | tf_op args[3]
  2.6 22.2 %shard_map.77 = (f32[1,16,1024]{2,1,0:T(8,128)}, f32[1,1,13]{2,1,0:T(1,128)}) custom-call(bf16[1,16,4096]{2,1,0:T(8,128)(2,1)} %template_ref.1, bf16[1,1,16,4096]{3,2,1,0:T(8,128)(2,1)} %science_ref.1, s32[4]{0:T(128)} %plan_ref.1, s32[6,2]{1,0:T(8,128)} %copy.8.orders_ref, f32[1,1]{1,0:T(1,128)S(6)} %copy.11.weight_ref, s32[1,1]{1,0:T(1,128)S(6)} %copy.12.inter_ref), custom_call_target="tpu_custom_call" | custom-call | tf_op jit(solution)/shard_map/pallas_call | solution.py:499
  24.8 0.0 copy-start.1
  24.8 1.5 %copy.13 = f32[1,16,1024]{2,1,0:T(8,128)} copy(f32[1,16,1024]{2,1,0:T(8,128)} %get-tuple-element.4) | data formatting | bytes 131072
  26.3 0.0 copy-done.1
  26.3 0.5 %copy.14 = f32[1,1,13]{2,1,0:T(1,128)} copy(f32[1,1,13]{2,1,0:T(1,128)S(1)} %copy-done.1) | data formatting | bytes 104
Async XLA Ops:
  1.3 0.7 %copy-start = (s32[6,2]{0,1:T(2,128)S(1)}, s32[6,2]{0,1:T(2,128)}, u32[]{:S(2)}) copy-start(s32[6,2]{0,1:T(2,128)} %param.9) | copy-start | bytes 148
  24.8 1.5 %copy-start.1 = (f32[1,1,13]{2,1,0:T(1,128)S(1)}, f32[1,1,13]{2,1,0:T(1,128)}, u32[]{:S(2)}) copy-start(f32[1,1,13]{2,1,0:T(1,128)} %get-tuple-element.5) | copy-start | bytes 160

commit v2 on v1

--- a/solution.py
+++ b/solution.py
@@ -110,6 +110,7 @@
 
 
 LANES = 128
+VMEM_BYTES = 67043328
 WIDE = 256
 PAIRS = [(u, v) for u in range(NB) for v in range(u + 1)]
 MESH = pl.DeviceIdType.MESH
@@ -163,10 +164,12 @@
                     yield de * tiles + dt, (me + de) % expos, (tile + dt) % tiles
 
     barrier = pltpu.get_barrier_semaphore()
-    for _, e, t in others():
-        pl.semaphore_signal(
-            barrier, inc=1, device_id={"expo": e, "tile": t}, device_id_type=MESH
-        )
+    for d in range(1, expos):
+        peer = (me + d) % expos
+        pl.semaphore_signal(barrier, inc=1, device_id={"expo": peer}, device_id_type=MESH)
+    for d in (1, tiles - 1):
+        peer = (tile + d) % tiles
+        pl.semaphore_signal(barrier, inc=1, device_id={"tile": peer}, device_id_type=MESH)
 
     def source_start(e):
         return e * per - 1 + (expos - 1 - e) // (expos - 1) - e // (expos - 1)
@@ -190,7 +193,6 @@
         science_ref.at[0, 0, :, own_columns(me)], sbuf.at[me], local_sem.at[1]
     )
     mine_science.start()
-    pl.semaphore_wait(barrier, expos * tiles - 1)
 
     def template_copy(d, target, holder):
         return pltpu.make_async_remote_copy(
@@ -232,18 +234,11 @@
         def _():
             forward_copy(d, holder, 1).start()
 
-    for d in range(1, expos):
-        template_copy(d, (me + d) % expos, me).start()
-    mine.wait()
-    forward(0, me)
-    for d in range(1, expos):
-        science_copy(d, (me + d) % expos, me).start()
-
     position = lax.broadcasted_iota(jnp.int32, (1, LANES), 1).astype(jnp.float32) - HALF
     for k in range(NB):
         sigma = SIGMAS[k]
         for side, length in ((0, rows), (1, LANES)):
-            order = jnp.full((1, LANES), orders_ref[k, side], jnp.int32)
+            order = jnp.full((1, LANES), orders_ref[side, k], jnp.int32)
             line = taps(position, sigma, order)
             root = jnp.sqrt(jnp.sum(line * line, axis=1, keepdims=True))
             scale = 1.0 / root
@@ -254,14 +249,14 @@
                     - lax.broadcasted_iota(jnp.int32, shape, 0)
                     - rows
                 ).astype(jnp.float32)
-                band = taps(offset, sigma, jnp.full(shape, orders_ref[k, side], jnp.int32))
+                band = taps(offset, sigma, jnp.full(shape, orders_ref[side, k], jnp.int32))
                 row_band[k * rows : (k + 1) * rows, :] = (band * scale).astype(jnp.bfloat16)
             else:
                 shape = (LANES, LANES)
                 delta = lax.broadcasted_iota(jnp.int32, shape, 0) - lax.broadcasted_iota(
                     jnp.int32, shape, 1
                 )
-                column_order = jnp.full(shape, orders_ref[k, side], jnp.int32)
+                column_order = jnp.full(shape, orders_ref[side, k], jnp.int32)
                 zero = jnp.zeros(shape, jnp.bfloat16)
                 parts = {}
                 for kind in range(3):
@@ -275,6 +270,14 @@
                             jb * LANES : (jb + 1) * LANES,
                             cb * LANES : (cb + 1) * LANES,
                         ] = parts.get(jb - cb, zero)
+
+    pl.semaphore_wait(barrier, expos + 1)
+    for d in range(1, expos):
+        template_copy(d, (me + d) % expos, me).start()
+    mine.wait()
+    forward(0, me)
+    for d in range(1, expos):
+        science_copy(d, (me + d) % expos, me).start()
 
     for d in range(1, expos):
         holder = (me + expos - d) % expos
@@ -381,7 +384,7 @@
         stat_ref[used:LANES, :] = jnp.zeros((LANES - used, LANES), jnp.float32)
 
     reduced = jnp.sum(jnp.transpose(stat_ref[...]), axis=0, keepdims=True)
-    weight = weight_ref[0, 0] * inter_ref[0, 0].astype(jnp.float32)
+    weight = weight_ref[0] * inter_ref[0].astype(jnp.float32)
     rbuf[me, tile, :, :LANES] = reduced
     rbuf[me, tile, :, LANES:] = jnp.full((1, LANES), weight, jnp.float32)
 
@@ -483,6 +486,7 @@
         science.shape[1] == 1
         and template.shape[0] == 1
         and expos > 1
+        and tiles > 1
         and width % expos == 0
         and cols % WIDE == 0
         and rows % 16 == 0
@@ -491,10 +495,11 @@
     if not fits:
         return per_device(template, science, plan, orders, coadd_weight, intersection)
     span = cols + 4 * LANES
+    spare = 4 * rows * cols + (1 << 14)
     dims = (expos, tiles, rows, width, cols)
     dma = pltpu.SemaphoreType.DMA
-    anywhere = pl.BlockSpec(memory_space=pl.ANY)
     scalar = pl.BlockSpec(memory_space=pltpu.SMEM)
+    far = pl.BlockSpec(memory_space=pltpu.HBM)
     vector = pl.BlockSpec(memory_space=pltpu.VMEM)
     return pl.pallas_call(
         functools.partial(fused, dims),
@@ -502,7 +507,7 @@
             jax.ShapeDtypeStruct((1, rows, cols), jnp.float32),
             jax.ShapeDtypeStruct((1, 1, NU), jnp.float32),
         ),
-        in_specs=[anywhere, anywhere, scalar, scalar, scalar, scalar],
+        in_specs=[far, far, scalar, scalar, scalar, scalar],
         out_specs=(vector, vector),
         scratch_shapes=[
             pltpu.VMEM((expos, 3, rows, span), jnp.bfloat16),
@@ -522,8 +527,8 @@
             dma((expos * tiles,)),
             dma((expos * tiles,)),
         ],
-        compiler_params=pltpu.CompilerParams(collective_id=0, has_side_effects=True),
-    )(template, science, plan, orders, coadd_weight, intersection)
+        compiler_params=pltpu.CompilerParams(collective_id=0, has_side_effects=True, vmem_limit_bytes=VMEM_BYTES - spare),
+    )(template, science, plan, orders.T, coadd_weight[0], intersection[0])
 
 
 def solution(mesh):

time: 27.1 us -> 26.1 us (0.963)
  local copies, waits for them, and re-layouts: 2.68 us -> 1.99 us
  Pallas kernels: 22.2 us -> 21.9 us
    unnamed x7 -> x4, local copies, waits for them, and re-layouts: 2.68 us -> 1.99 us
where the time goes in v2:
time: 26.1 us; the launch traced here: 25.9 us
  Pallas kernels  21.9 us (84%)
  local copies, waits for them, and re-layouts  1.99 us (8%)
  between operations  1.94 us (7%)
    pallas_call x1, Pallas kernels, window(): pl.pallas_call(functools.partial(fused, dims), out_shape=(jax.ShapeDtypeS...  21.9 us
    unnamed x4, local copies, waits for them, and re-layouts  1.99 us

profile of v2, /device:TPU:0, one launch (start us, length us, event | category | flops | bytes accessed | tf_op | source)
XLA Modules:
  0.0 25.9 jit_solution(12154702401146273827)
XLA Ops:
  1.9 21.9 %shard_map.77 = (f32[1,16,1024]{2,1,0:T(8,128)}, f32[1,1,13]{2,1,0:T(1,128)}) custom-call(bf16[1,16,4096]{2,1,0:T(8,128)(2,1)} %template_ref.1, bf16[1,1,16,4096]{3,2,1,0:T(8,128)(2,1)} %science_ref.1, s32[4]{0:T(128)} %plan_ref.1, s32[2,6]{1,0:T(2,128)} %bitcast.5, f32[1]{0:T(128)} %bitcast.3.weight_ref, s32[1]{0:T(128)} %bitcast.4.inter_ref), custom_call_target="tpu_custom_call" | custom-call | tf_op jit(solution)/shard_map/pallas_call | solution.py:504
  23.9 0.0 copy-start
  23.9 1.5 %copy.12 = f32[1,16,1024]{2,1,0:T(8,128)} copy(f32[1,16,1024]{2,1,0:T(8,128)} %get-tuple-element.4) | data formatting | bytes 131072
  25.4 0.0 copy-done
  25.4 0.5 %copy.13 = f32[1,1,13]{2,1,0:T(1,128)} copy(f32[1,1,13]{2,1,0:T(1,128)S(1)} %copy-done) | data formatting | bytes 104
Async XLA Ops:
  23.9 1.5 %copy-start = (f32[1,1,13]{2,1,0:T(1,128)S(1)}, f32[1,1,13]{2,1,0:T(1,128)}, u32[]{:S(2)}) copy-start(f32[1,1,13]{2,1,0:T(1,128)} %get-tuple-element.5) | copy-start | bytes 160

commit v3 on v2

--- a/solution.py
+++ b/solution.py
@@ -384,9 +384,9 @@
         stat_ref[used:LANES, :] = jnp.zeros((LANES - used, LANES), jnp.float32)
 
     reduced = jnp.sum(jnp.transpose(stat_ref[...]), axis=0, keepdims=True)
-    weight = weight_ref[0] * inter_ref[0].astype(jnp.float32)
+    weight = weight_ref[...] * inter_ref[...].astype(jnp.float32)
     rbuf[me, tile, :, :LANES] = reduced
-    rbuf[me, tile, :, LANES:] = jnp.full((1, LANES), weight, jnp.float32)
+    rbuf[me, tile, :, LANES:] = jnp.broadcast_to(weight, (1, LANES))
 
     def stat_copy(index, e, t, to_e, to_t):
         return pltpu.make_async_remote_copy(
@@ -495,7 +495,7 @@
     if not fits:
         return per_device(template, science, plan, orders, coadd_weight, intersection)
     span = cols + 4 * LANES
-    spare = 4 * rows * cols + (1 << 14)
+    spare = 10368 * 1024
     dims = (expos, tiles, rows, width, cols)
     dma = pltpu.SemaphoreType.DMA
     scalar = pl.BlockSpec(memory_space=pltpu.SMEM)
@@ -507,7 +507,7 @@
             jax.ShapeDtypeStruct((1, rows, cols), jnp.float32),
             jax.ShapeDtypeStruct((1, 1, NU), jnp.float32),
         ),
-        in_specs=[far, far, scalar, scalar, scalar, scalar],
+        in_specs=[far, far, scalar, scalar, vector, vector],
         out_specs=(vector, vector),
         scratch_shapes=[
             pltpu.VMEM((expos, 3, rows, span), jnp.bfloat16),
@@ -528,7 +528,7 @@
             dma((expos * tiles,)),
         ],
         compiler_params=pltpu.CompilerParams(collective_id=0, has_side_effects=True, vmem_limit_bytes=VMEM_BYTES - spare),
-    )(template, science, plan, orders.T, coadd_weight[0], intersection[0])
+    )(template, science, plan, orders.T, coadd_weight, intersection)
 
 
 def solution(mesh):

time: 26.1 us -> 25.1 us (0.962)
  Pallas kernels: 21.9 us -> 21.2 us
    pallas_call x1, Pallas kernels: 21.9 us -> 21.2 us  [window(): pl.pallas_call(functools.partial(fused, dims), out_shape=(jax.ShapeDtypeS...]
    unnamed x4 -> x6, local copies, waits for them, and re-layouts: 1.99 us -> 1.81 us
where the time goes in v3:
time: 25.1 us; the launch traced here: 24.9 us
  Pallas kernels  21.2 us (84%)
  between operations  1.95 us (8%)
  local copies, waits for them, and re-layouts  1.81 us (7%)
    pallas_call x1, Pallas kernels, window(): pl.pallas_call(functools.partial(fused, dims), out_shape=(jax.ShapeDtypeS...  21.2 us
    unnamed x6, local copies, waits for them, and re-layouts  1.81 us

profile of v3, /device:TPU:0, one launch (start us, length us, event | category | flops | bytes accessed | tf_op | source)
XLA Modules:
  0.0 24.9 jit_solution(1873098592985767726)
XLA Ops:
  1.9 0.0 copy-start
  1.9 0.0 copy-start.1
  1.9 0.7 %copy-done = s32[6,2]{0,1:T(2,128)S(1)} copy-done((s32[6,2]{0,1:T(2,128)S(1)}, s32[6,2]{0,1:T(2,128)}, u32[]{:S(2)}) %copy-start) | copy-done | bytes 72
  2.6 0.0 copy-done.1
  2.6 21.2 %shard_map.77 = (f32[1,16,1024]{2,1,0:T(8,128)S(1)}, f32[1,1,13]{2,1,0:T(1,128)S(1)}) custom-call(bf16[1,16,4096]{2,1,0:T(8,128)(2,1)} %template_ref.1, bf16[1,1,16,4096]{3,2,1,0:T(8,128)(2,1)} %science_ref.1, s32[4]{0:T(128)S(1)} %copy-done.1, s32[2,6]{1,0:T(2,128)S(1)} %bitcast.1, f32[1,1]{1,0:T(1,128)S(6)} %copy.10.weight_ref, s32[1,1]{1,0:T(1,128)S(6)} %copy.11.inter_ref), custom_call_target="tpu_custom_call" | custom-call | tf_op jit(solution)/shard_map/pallas_call | solution.py:504
  23.8 0.6 %copy.12 = f32[1,16,1024]{2,1,0:T(8,128)} copy(f32[1,16,1024]{2,1,0:T(8,128)S(1)} %get-tuple-element.4) | data formatting | bytes 131072
  24.4 0.5 %copy.13 = f32[1,1,13]{2,1,0:T(1,128)} copy(f32[1,1,13]{2,1,0:T(1,128)S(1)} %get-tuple-element.5) | data formatting | bytes 104
Async XLA Ops:
  1.9 0.7 %copy-start = (s32[6,2]{0,1:T(2,128)S(1)}, s32[6,2]{0,1:T(2,128)}, u32[]{:S(2)}) copy-start(s32[6,2]{0,1:T(2,128)} %param.9) | copy-start | bytes 148
  1.9 0.7 %copy-start.1 = (s32[4]{0:T(128)S(1)}, s32[4]{0:T(128)}, u32[]{:S(2)}) copy-start(s32[4]{0:T(128)} %plan_ref.1) | copy-start | bytes 52

commit v4 on v3

--- a/solution.py
+++ b/solution.py
@@ -272,14 +272,14 @@
                         ] = parts.get(jb - cb, zero)
 
     pl.semaphore_wait(barrier, expos + 1)
-    for d in range(1, expos):
+    for d in reversed(range(1, expos)):
         template_copy(d, (me + d) % expos, me).start()
     mine.wait()
     forward(0, me)
     for d in range(1, expos):
         science_copy(d, (me + d) % expos, me).start()
 
-    for d in range(1, expos):
+    for d in reversed(range(1, expos)):
         holder = (me + expos - d) % expos
         template_copy(d, me, holder).wait_recv()
         forward(d, holder)

time: 25.1 us -> 24 us (0.956)
  Pallas kernels: 21.2 us -> 20.1 us
    pallas_call x1, Pallas kernels: 21.2 us -> 20.1 us  [window(): pl.pallas_call(functools.partial(fused, dims), out_shape=(jax.ShapeDtypeS...]
where the time goes in v4:
time: 24 us; the launch traced here: 23.8 us
  Pallas kernels  20.1 us (84%)
  between operations  1.95 us (8%)
  local copies, waits for them, and re-layouts  1.81 us (8%)
    pallas_call x1, Pallas kernels, window(): pl.pallas_call(functools.partial(fused, dims), out_shape=(jax.ShapeDtypeS...  20.1 us
    unnamed x6, local copies, waits for them, and re-layouts  1.81 us

profile of v4, /device:TPU:0, one launch (start us, length us, event | category | flops | bytes accessed | tf_op | source)
XLA Modules:
  0.0 23.8 jit_solution(1620683842319845226)
XLA Ops:
  1.9 0.0 copy-start
  1.9 0.0 copy-start.1
  1.9 0.7 %copy-done = s32[6,2]{0,1:T(2,128)S(1)} copy-done((s32[6,2]{0,1:T(2,128)S(1)}, s32[6,2]{0,1:T(2,128)}, u32[]{:S(2)}) %copy-start) | copy-done | bytes 72
  2.6 0.0 copy-done.1
  2.6 20.1 %shard_map.77 = (f32[1,16,1024]{2,1,0:T(8,128)S(1)}, f32[1,1,13]{2,1,0:T(1,128)S(1)}) custom-call(bf16[1,16,4096]{2,1,0:T(8,128)(2,1)} %template_ref.1, bf16[1,1,16,4096]{3,2,1,0:T(8,128)(2,1)} %science_ref.1, s32[4]{0:T(128)S(1)} %copy-done.1, s32[2,6]{1,0:T(2,128)S(1)} %bitcast.1, f32[1,1]{1,0:T(1,128)S(6)} %copy.10.weight_ref, s32[1,1]{1,0:T(1,128)S(6)} %copy.11.inter_ref), custom_call_target="tpu_custom_call" | custom-call | tf_op jit(solution)/shard_map/pallas_call | solution.py:504
  22.7 0.6 %copy.12 = f32[1,16,1024]{2,1,0:T(8,128)} copy(f32[1,16,1024]{2,1,0:T(8,128)S(1)} %get-tuple-element.4) | data formatting | bytes 131072
  23.3 0.5 %copy.13 = f32[1,1,13]{2,1,0:T(1,128)} copy(f32[1,1,13]{2,1,0:T(1,128)S(1)} %get-tuple-element.5) | data formatting | bytes 104
Async XLA Ops:
  1.9 0.7 %copy-start = (s32[6,2]{0,1:T(2,128)S(1)}, s32[6,2]{0,1:T(2,128)}, u32[]{:S(2)}) copy-start(s32[6,2]{0,1:T(2,128)} %param.9) | copy-start | bytes 148
  1.9 0.7 %copy-start.1 = (s32[4]{0:T(128)S(1)}, s32[4]{0:T(128)}, u32[]{:S(2)}) copy-start(s32[4]{0:T(128)} %plan_ref.1) | copy-start | bytes 52
